TPU v7x, 32 devices: a whole 2x2x4 slice. The times are simulated.
32 devices in a mesh: flow: 2 (over x), cross: 4 (over z), depth: 4 (over y, core).
Axes of the slice: x: 2, y: 2, z: 4, core: 2. Of those that a mesh axis runs over, the one named last changes fastest.
Arguments:
- fluid_offsets: float32 [3, 2, 16, 16, 128], P(None, 'flow', 'cross', 'depth'), may hold values from 0 to 1
- source: float32 [2, 16, 16, 128], P('flow', 'cross', 'depth'), may hold values from -6 to 6
- marker_offsets: float32 [512, 16, 3, 128], P(('flow', 'cross', 'depth')), may hold values from 0 to 1
- marker_normals: float32 [512, 16, 3, 128], P(('flow', 'cross', 'depth')), may hold values from -6 to 6
- dest_tile: int32 [512, 16, 1], P(('flow', 'cross', 'depth')), may hold values from 0 to 7; in each aligned block of 256 rows (0 to 255, 256 to 511, ..., all dimensions but the last counted through in order) at most 64 rows name the same one
- cell_index: int32 [512, 16], P(('flow', 'cross', 'depth')), may hold values from 0 to 15
- grain_velocity: float32 [512, 3], P(('flow', 'cross', 'depth')), may hold values from -6 to 6
- grain_mass: float32 [512], P(('flow', 'cross', 'depth')), may hold values from 0.5 to 4
Outputs:
- pressure: float32 [2, 16, 16, 128], P('flow', 'cross', 'depth')
- velocity_out: float32 [512, 3], P(('flow', 'cross', 'depth'))
Inputs may be any that keep to these rules, and one draw needn't show every extreme that they name: `dest_tile`: in the rows of one device at most 64 marker blocks name the same tile.
All inputs are finite; a program needn't handle non-finite values.
Results may differ from a plain program's by a relative error of at most 0.0003.
Values sent between devices are 32-bit elements; how exact they have to be, the bound alone decides.
A program may use at most 64 MiB of HBM per device.

v0:
```python
import jax
import jax.numpy as jnp
from jax import lax
from jax.sharding import PartitionSpec as P

ITERS = 4
STEPS = 2


NEIGHBOURS = ((0, 0, 0), (1, 0, 0), (-1, 0, 0), (0, 1, 0), (0, -1, 0), (0, 0, 1), (0, 0, -1))
STIFFEN = 0.5
STEP_TIME = 0.05
PER_PARTICLE = 1.0 / 128.0


def padded_2(shard, sides, width):
    for axis, dim in sides:
        devices, length = (lax.axis_size(axis), shard.shape[dim])
        up = [(i, (i + 1) % devices) for i in range(devices)]
        down = [(j, i) for i, j in up]
        last = lax.slice_in_dim(shard, length - width, length, axis=dim)
        initial = lax.slice_in_dim(shard, 0, width, axis=dim)
        before = lax.ppermute(last, axis, up)
        after = lax.ppermute(initial, axis, down)
        shard = jnp.concatenate([before, shard, after], axis=dim)
    return shard


def pair_kernel(own_off, near_off, offset, values):
    total = None
    for component in range(3):
        gap = (near_off[component] + float(offset[component]))[..., None, :] - own_off[component][
            ..., :, None
        ]
        total = gap * gap if total is None else total + gap * gap
    weight = jnp.exp(-total) * PER_PARTICLE
    return jnp.sum(weight * values[..., None, :], axis=-1)


def marker_weights(fluid_rows, positions):
    total = None
    for component in range(3):
        gap = fluid_rows[:, component, :, None] - positions[:, component, None, :]
        total = gap * gap if total is None else total + gap * gap
    return jnp.exp(-total) * PER_PARTICLE


def neighbour_sum(padded_off, own_off, padded_val):
    size_x, size_y, size_z = (own_off.shape[1], own_off.shape[2], own_off.shape[3])
    total = jnp.zeros(own_off.shape[1:], jnp.float32)
    for offset in NEIGHBOURS:
        low_x, low_y, low_z = (1 + offset[0], 1 + offset[1], 1 + offset[2])
        near_off = padded_off[
            :, low_x : low_x + size_x, low_y : low_y + size_y, low_z : low_z + size_z
        ]
        if padded_val is None:
            values = jnp.ones(own_off.shape[1:], jnp.float32)
        else:
            values = padded_val[
                low_x : low_x + size_x, low_y : low_y + size_y, low_z : low_z + size_z
            ]
        total = total + pair_kernel(own_off, near_off, offset, values)
    return total


def marker_pass(fluid_rows, geometry, motion, target, keeper, field_rows, toward_fluid):
    slot_count = geometry.shape[0]
    group = 32
    group_count = slot_count // group

    def one_group(pieces):
        shape_rows, moving, where, keep_rows = pieces
        positions = shape_rows[:, 0:3, :] + moving[:, 0:3, None]
        weight = marker_weights(fluid_rows[where], positions)
        if toward_fluid:
            rate = (
                shape_rows[:, 3] * moving[:, 3, None]
                + shape_rows[:, 4] * moving[:, 4, None]
                + shape_rows[:, 5] * moving[:, 5, None]
            )
            result = jnp.sum(weight * rate[:, None, :], axis=-1)
        else:
            result = jnp.sum(weight * field_rows[where][:, :, None], axis=1)
        return result * keep_rows[:, None]

    pieces = (
        geometry.reshape(group_count, group, 6, 128),
        motion.reshape(group_count, group, 6),
        target.reshape(group_count, group),
        keeper.reshape(group_count, group),
    )
    return lax.map(one_group, pieces).reshape(slot_count, 128)


def send_markers(geo_buffer, motion_buffer, cell_buffer):
    return (
        lax.all_to_all(geo_buffer, ("flow", "cross"), split_axis=0, concat_axis=0, tiled=True),
        lax.all_to_all(motion_buffer, ("flow", "cross"), split_axis=0, concat_axis=0, tiled=True),
        lax.all_to_all(cell_buffer, ("flow", "cross"), split_axis=0, concat_axis=0, tiled=True),
    )


def paired_sums(residual, precond, image):
    return lax.psum(
        (jnp.sum(residual * precond), jnp.sum(image * precond)), ("flow", "cross", "depth")
    )


def per_device(
    fluid_offsets,
    source,
    marker_offsets,
    marker_normals,
    dest_tile,
    cell_index,
    grain_velocity,
    grain_mass,
):
    cell_count = source.shape[0] * source.shape[1] * source.shape[2]
    padded_off = padded_2(fluid_offsets, (("flow", 1), ("cross", 2), ("depth", 3)), 1)
    rowsum = neighbour_sum(padded_off, fluid_offsets, None)
    diagonal = STIFFEN + rowsum - PER_PARTICLE

    def operate(field):
        padded = padded_2(field, (("flow", 0), ("cross", 1), ("depth", 2)), 1)
        return (STIFFEN + rowsum) * field - neighbour_sum(padded_off, fluid_offsets, padded)

    tile_count = lax.axis_size("flow") * lax.axis_size("cross")
    block_rows = dest_tile.shape[0] * dest_tile.shape[1]
    per_grain = dest_tile.shape[1]
    capacity = max(2, 2 * block_rows // tile_count)
    slot_count = tile_count * capacity
    destination = dest_tile.reshape(block_rows)
    member = (destination[:, None] == jnp.arange(tile_count, dtype=jnp.int32)[None, :]).astype(
        jnp.int32
    )
    order_rank = jnp.sum(member * jnp.cumsum(member, axis=0), axis=1) - 1
    slot_index = destination * capacity + order_rank
    geometry = jnp.concatenate([marker_offsets, marker_normals], axis=2).reshape(block_rows, 6, 128)
    geo_buffer = (
        jnp.zeros((slot_count, 6, 128), jnp.float32)
        .at[slot_index]
        .set(geometry)
        .reshape(tile_count, capacity, 6, 128)
    )
    cell_buffer = (
        jnp.full((slot_count,), -1, jnp.int32)
        .at[slot_index]
        .set(cell_index.reshape(block_rows))
        .reshape(tile_count, capacity)
    )
    fluid_rows = jnp.transpose(fluid_offsets, (1, 2, 3, 0, 4)).reshape(cell_count, 3, 128)
    cell_ids = jnp.arange(cell_count, dtype=jnp.int32)
    velocity = grain_velocity
    displace = jnp.zeros(grain_velocity.shape, jnp.float32)
    pressure = jnp.zeros(source.shape, jnp.float32)
    got_geometry = None
    got_cells = None
    for step_index in range(STEPS):
        motion_rows = jnp.repeat(jnp.concatenate([displace, velocity], axis=1), per_grain, axis=0)
        motion_buffer = (
            jnp.zeros((slot_count, 6), jnp.float32)
            .at[slot_index]
            .set(motion_rows)
            .reshape(tile_count, capacity, 6)
        )
        got_geometry, got_motion, got_cells = send_markers(geo_buffer, motion_buffer, cell_buffer)
        slot_geometry = got_geometry.reshape(slot_count, 6, 128)
        slot_motion = got_motion.reshape(slot_count, 6)
        slot_cells = got_cells.reshape(slot_count)
        occupied = slot_cells >= 0
        safe_cells = jnp.where(occupied, slot_cells, 0)
        keeper = occupied.astype(jnp.float32)
        added = marker_pass(fluid_rows, slot_geometry, slot_motion, safe_cells, keeper, None, True)
        membership = ((safe_cells[:, None] == cell_ids[None, :]) & occupied[:, None]).astype(
            jnp.float32
        )
        gathered = jnp.einsum("sc,si->ci", membership, added, precision=lax.Precision.HIGHEST)
        right_side = source + gathered.reshape(source.shape)
        solution = pressure
        residual = right_side - operate(solution)
        precond = residual / diagonal
        image = operate(precond)
        norm_now, product = paired_sums(residual, precond, image)
        alpha = norm_now / product
        direction, along = (precond, image)
        for iteration in range(ITERS):
            solution = solution + alpha * direction
            residual = residual - alpha * along
            if iteration + 1 < ITERS:
                precond = residual / diagonal
                image = operate(precond)
                norm_next, product = paired_sums(residual, precond, image)
                ratio = norm_next / norm_now
                alpha = norm_next / (product - ratio * norm_next / alpha)
                direction = precond + ratio * direction
                along = image + ratio * along
                norm_now = norm_next
        pressure = solution
        felt = marker_pass(
            fluid_rows,
            slot_geometry,
            slot_motion,
            safe_cells,
            keeper,
            pressure.reshape(cell_count, 128),
            False,
        )
        returned = lax.all_to_all(
            felt.reshape(tile_count, capacity, 128),
            ("flow", "cross"),
            split_axis=0,
            concat_axis=0,
            tiled=True,
        )
        own_felt = returned.reshape(slot_count, 128)[slot_index]
        block_force = jnp.sum(
            marker_normals.reshape(block_rows, 3, 128) * own_felt[:, None, :], axis=-1
        )
        grain_force = jnp.sum(block_force.reshape(-1, per_grain, 3), axis=1)
        velocity = velocity + STEP_TIME * grain_force / grain_mass[:, None]
        displace = displace + STEP_TIME * velocity
    return (pressure, velocity)


def solution(mesh):
    return jax.shard_map(
        per_device,
        mesh=mesh,
        in_specs=(
            P(None, "flow", "cross", "depth", None),
            P("flow", "cross", "depth", None),
            P(("flow", "cross", "depth"), None, None, None),
            P(("flow", "cross", "depth"), None, None, None),
            P(("flow", "cross", "depth"), None, None),
            P(("flow", "cross", "depth"), None),
            P(("flow", "cross", "depth"), None),
            P(("flow", "cross", "depth")),
        ),
        out_specs=(P("flow", "cross", "depth", None), P(("flow", "cross", "depth"), None)),
        check_vma=False,
    )
```

profile of v0, /device:TPU:0, one launch (start us, length us, event | category | flops | bytes accessed | tf_op | source)
XLA Modules:
  0.0 913.5 jit_solution(16834069757797087143)
XLA Ops:
  0.6 3.0 collective-permute-start.6
  12.4 6.3 all-to-all-start
  21.3 6.9 scatter_fusion
  32.0 6.0 all-to-all-start.2
  38.8 3.9 collective-permute-start.8
  44.1 4.1 collective-permute-done.9
  48.7 3.6 all-to-all-start.1
  53.8 3.8 collective-permute-start.2
  57.6 23.7 %collective-permute-done.2 = f32[3,3,1,4,128]{4,3,2,1,0:T(4,128)S(1)} collective-permute-done((f32[3,3,1,4,128]{4,3,2,1,0:T(4,128)S(1)}, f32[3,3,1,4,128]{4,3,2,1,0:T(4,128)S(1)}, u32[]{:S(2)}, u32[]{:S(2)}) %collective-permute-start.2) | collective-permute-done | bytes 18464 | tf_op jit(solution)/shard_map/ppermute | solution.py:24
  81.3 2.9 collective-permute-done.3
  89.9 4.8 multiply_reduce_fusion.79
  95.1 57.6 %while.40 = (s32[]{:T(128)}, f32[16,32,128]{2,1,0:T(8,128)S(1)}, s32[16,32]{1,0:T(8,128)S(1)}, f32[16,3,128]{2,1,0:T(4,128)S(1)}, f32[16,32,6,128]{3,1,2,0:T(8,1...) while((s32[]{:T(128)}, f32[16,32,128]{2,1,0:T(8,128)S(1)}, ...), condition=%wide.region_8.9_spmd, body=%wide.region_6.8_spmd.sunk | while | flops 5805154 | bytes 828521 | solution.py:92
  96.0 2.6 multiply_reduce_fusion.102
  114.0 2.6 multiply_reduce_fusion.102
  117.6 2.6 multiply_reduce_fusion.102
  159.6 6.1 collective-permute-start.15
  174.5 3.0 multiply_reduce_fusion.65
  178.1 39.2 %all-reduce.8 = (f32[]{:T(128)}, f32[]{:T(128)}) all-reduce(f32[]{:T(128)} %get-tuple-element.418, f32[]{:T(128)} %get-tuple-element.417), channel_id=1, replica_groups=mesh['flow'=2,'cross'=4,'depth'=4] {'flow','cross','depth'}, use_global_device_ids=true, to_apply=%region_24.25 | all-reduce | flops 2 | bytes 16 | tf_op jit(solution)/shard_map/psum | solution.py:104
  228.4 4.1 collective-permute-done.21
  237.9 3.0 multiply_reduce_fusion.58
  241.5 37.4 %all-reduce.7 = (f32[]{:T(128)}, f32[]{:T(128)}) all-reduce(f32[]{:T(128)} %get-tuple-element.416, f32[]{:T(128)} %get-tuple-element.415), channel_id=1, replica_groups=mesh['flow'=2,'cross'=4,'depth'=4] {'flow','cross','depth'}, use_global_device_ids=true, to_apply=%region_35.36 | all-reduce | flops 2 | bytes 16 | tf_op jit(solution)/shard_map/psum | solution.py:104
  293.9 3.2 collective-permute-done.27
  302.5 3.0 multiply_reduce_fusion.51
  306.1 37.6 %all-reduce.6 = (f32[]{:T(128)}, f32[]{:T(128)}) all-reduce(f32[]{:T(128)} %get-tuple-element.414, f32[]{:T(128)} %get-tuple-element.413), channel_id=1, replica_groups=mesh['flow'=2,'cross'=4,'depth'=4] {'flow','cross','depth'}, use_global_device_ids=true, to_apply=%region_46.47 | all-reduce | flops 2 | bytes 16 | tf_op jit(solution)/shard_map/psum | solution.py:104
  357.9 3.5 collective-permute-done.33
  366.9 3.0 multiply_reduce_fusion.44
  370.5 37.3 %all-reduce.5 = (f32[]{:T(128)}, f32[]{:T(128)}) all-reduce(f32[]{:T(128)} %get-tuple-element.412, f32[]{:T(128)} %get-tuple-element.411), channel_id=1, replica_groups=mesh['flow'=2,'cross'=4,'depth'=4] {'flow','cross','depth'}, use_global_device_ids=true, to_apply=%region_57.58 | all-reduce | flops 2 | bytes 16 | tf_op jit(solution)/shard_map/psum | solution.py:104
  421.3 74.1 %while.41 = (s32[]{:T(128)}, f32[16,32,128]{2,1,0:T(8,128)}, s32[16,32]{1,0:T(8,128)S(1)}, f32[16,3,128]{2,1,0:T(4,128)S(1)}, f32[16,32,6,128]{3,1,2,0:T(8,128)S...) while((s32[]{:T(128)}, f32[16,32,128]{2,1,0:T(8,128)}, ...), condition=%wide.region_69.70_spmd, body=%wide.region_67.69_spmd.sunk | while | flops 5784674 | bytes 827629 | solution.py:92
  495.5 4.5 all-to-all-start.3
  503.4 3.0 multiply_reduce_fusion.37
  511.7 3.9 all-to-all-start.4
  517.8 4.4 all-to-all-done.4
  523.0 57.6 %while.42 = (s32[]{:T(128)}, f32[16,32,128]{2,1,0:T(8,128)S(1)}, s32[16,32]{1,0:T(8,128)S(1)}, f32[16,3,128]{2,1,0:T(4,128)S(1)}, f32[16,32,6,128]{3,1,2,0:T(8,1...) while((s32[]{:T(128)}, f32[16,32,128]{2,1,0:T(8,128)S(1)}, ...), condition=%wide.region_74.75_spmd, body=%wide.region_72.74_spmd.sunk | while | flops 5805154 | bytes 828521 | solution.py:92
  527.5 2.6 multiply_reduce_fusion.104
  531.1 2.6 multiply_reduce_fusion.104
  596.5 3.0 multiply_reduce_fusion.30
  600.1 38.7 %all-reduce.4 = (f32[]{:T(128)}, f32[]{:T(128)}) all-reduce(f32[]{:T(128)} %get-tuple-element.410, f32[]{:T(128)} %get-tuple-element.409), channel_id=1, replica_groups=mesh['flow'=2,'cross'=4,'depth'=4] {'flow','cross','depth'}, use_global_device_ids=true, to_apply=%region_83.84 | all-reduce | flops 2 | bytes 16 | tf_op jit(solution)/shard_map/psum | solution.py:104
  650.1 3.2 collective-permute-done.51
  658.8 3.0 multiply_reduce_fusion.23
  662.5 37.6 %all-reduce.3 = (f32[]{:T(128)}, f32[]{:T(128)}) all-reduce(f32[]{:T(128)} %get-tuple-element.408, f32[]{:T(128)} %get-tuple-element.407), channel_id=1, replica_groups=mesh['flow'=2,'cross'=4,'depth'=4] {'flow','cross','depth'}, use_global_device_ids=true, to_apply=%region_94.95 | all-reduce | flops 2 | bytes 16 | tf_op jit(solution)/shard_map/psum | solution.py:104
  714.7 3.5 collective-permute-done.57
  723.9 3.0 multiply_reduce_fusion.16
  727.5 37.3 %all-reduce.2 = (f32[]{:T(128)}, f32[]{:T(128)}) all-reduce(f32[]{:T(128)} %get-tuple-element.406, f32[]{:T(128)} %get-tuple-element.405), channel_id=1, replica_groups=mesh['flow'=2,'cross'=4,'depth'=4] {'flow','cross','depth'}, use_global_device_ids=true, to_apply=%region_105.106 | all-reduce | flops 2 | bytes 16 | tf_op jit(solution)/shard_map/psum | solution.py:104
  779.2 3.2 collective-permute-done.63
  787.9 3.0 multiply_reduce_fusion.9
  791.6 37.6 %all-reduce.1 = (f32[]{:T(128)}, f32[]{:T(128)}) all-reduce(f32[]{:T(128)} %get-tuple-element.404, f32[]{:T(128)} %get-tuple-element.403), channel_id=1, replica_groups=mesh['flow'=2,'cross'=4,'depth'=4] {'flow','cross','depth'}, use_global_device_ids=true, to_apply=%region_116.117 | all-reduce | flops 2 | bytes 16 | tf_op jit(solution)/shard_map/psum | solution.py:104
  833.0 64.7 %while.43 = (s32[]{:T(128)}, f32[16,32,128]{2,1,0:T(8,128)S(1)}, s32[16,32]{1,0:T(8,128)S(1)}, f32[16,3,128]{2,1,0:T(4,128)S(1)}, f32[16,32,6,128]{3,1,2,0:T(8,1...) while((s32[]{:T(128)}, f32[16,32,128]{2,1,0:T(8,128)S(1)}, ...), condition=%wide.region_128.129_spmd, body=%wide.region_126.128_spmd.sunk | while | flops 5784674 | bytes 827505 | solution.py:92
  897.7 14.0 %all_to_all.36 = f32[8,64,128]{2,1,0:T(8,128)S(1)} all-to-all(f32[8,64,128]{2,1,0:T(8,128)S(1)} %bitcast.582), channel_id=1, replica_groups=mesh['flow'=2,'cross'=4,'depth'=4] {'flow','cross'}, dimensions={0} | all-to-all | bytes 524288 | tf_op jit(solution)/shard_map/all_to_all | solution.py:209
  (1142 shorter events, 415.4 us)
Async XLA Ops:
  0.6 38.2 %collective-permute-start.6 = (f32[1,4,4,128]{3,2,1,0:T(4,128)S(1)}, f32[1,4,4,128]{3,2,1,0:T(4,128)S(1)}, u32[]{:S(2)}, u32[]{:S(2)}) collective-permute-start(f32[1,4,4,128]{3,2,1,0:T(4,128)S(1)} %broadcast_in_dim.20), channel_id=1, source_target_pairs={{16,0},{0,16},{17,1},{1,17},{18,2},{2,18},{19,3},{3,19},{20,4},{4,... | collective-permute-start | bytes 24584 | tf_op jit(solution)/shard_map/ppermute | solution.py:24
  3.7 35.2 %collective-permute-start.7 = (f32[1,4,4,128]{3,2,1,0:T(4,128)S(1)}, f32[1,4,4,128]{3,2,1,0:T(4,128)S(1)}, u32[]{:S(2)}, u32[]{:S(2)}) collective-permute-start(f32[1,4,4,128]{3,2,1,0:T(4,128)S(1)} %broadcast_in_dim.20), channel_id=1, source_target_pairs={{0,16},{16,0},{1,17},{17,1},{2,18},{18,2},{3,19},{19,3},{4,20},{20... | collective-permute-start | bytes 24584 | tf_op jit(solution)/shard_map/ppermute | solution.py:23
  3.8 50.0 %collective-permute-start.1 = (f32[3,1,4,4,128]{4,3,2,1,0:T(4,128)}, f32[3,1,4,4,128]{4,3,2,1,0:T(4,128)S(1)}, u32[]{:S(2)}, u32[]{:S(2)}) collective-permute-start(f32[3,1,4,4,128]{4,3,2,1,0:T(4,128)} %param.16), channel_id=1, source_target_pairs={{0,16},{16,0},{1,17},{17,1},{2,18},{18,2},{3,19},{19,3},{4,20},{20... | collective-permute-start | bytes 73736 | tf_op jit(solution)/shard_map/ppermute | solution.py:23
  5.7 48.1 %collective-permute-start = (f32[3,1,4,4,128]{4,3,2,1,0:T(4,128)}, f32[3,1,4,4,128]{4,3,2,1,0:T(4,128)S(1)}, u32[]{:S(2)}, u32[]{:S(2)}) collective-permute-start(f32[3,1,4,4,128]{4,3,2,1,0:T(4,128)} %param.16), channel_id=1, source_target_pairs={{16,0},{0,16},{17,1},{1,17},{18,2},{2,18},{19,3},{3,19},{20,4},{4,... | collective-permute-start | bytes 73736 | tf_op jit(solution)/shard_map/ppermute | solution.py:24
  12.4 19.5 %all-to-all-start = ((s32[8,1,64]{2,1,0:T(1,128)}), s32[8,1,64]{2,1,0:T(1,128)S(1)}, u32[]{:S(2)}, u32[]{:S(2)}) async-start(s32[8,1,64]{2,1,0:T(1,128)} %all_to_all.23), calls=%async_computation | async-start | bytes 8192 | tf_op jit(solution)/shard_map/all_to_all | solution.py:99
  32.0 16.7 %all-to-all-start.2 = ((f32[8,1,384]{2,1,0:T(1,128)}), f32[8,1,384]{2,1,0:T(1,128)S(1)}, u32[]{:S(2)}, u32[]{:S(2)}) async-start(f32[8,1,384]{2,1,0:T(1,128)} %reshape.2467), calls=%async_computation.2 | async-start | bytes 24576 | tf_op jit(solution)/shard_map/all_to_all | solution.py:98
  38.8 5.2 collective-permute-start.8
  42.7 5.4 collective-permute-start.9
  48.2 5.5 collective-permute-start.10
  48.2 5.5 collective-permute-start.11
  48.7 46.0 %all-to-all-start.1 = ((f32[8,64,6,128]{3,1,2,0:T(8,128)}), f32[8,64,6,128]{3,1,2,0:T(8,128)S(1)}, u32[]{:S(2)}, u32[]{:S(2)}) async-start(f32[8,64,6,128]{3,1,2,0:T(8,128)} %copy.100), calls=%async_computation.1 | async-start | bytes 3145728 | tf_op jit(solution)/shard_map/all_to_all | solution.py:97
  53.8 27.5 %collective-permute-start.2 = (f32[3,3,1,4,128]{4,3,2,1,0:T(4,128)S(1)}, f32[3,3,1,4,128]{4,3,2,1,0:T(4,128)S(1)}, u32[]{:S(2)}, u32[]{:S(2)}) collective-permute-start(f32[3,3,1,4,128]{4,3,2,1,0:T(4,128)S(1)} %get-tuple-element.576), channel_id=1, source_target_pairs={{4,0},{8,4},{12,8},{0,12},{5,1},{9,5},{13,9},{1,13},{6,2},{10,6},{... | collective-permute-start | bytes 55304 | tf_op jit(solution)/shard_map/ppermute | solution.py:24
  57.6 26.6 %collective-permute-start.3 = (f32[3,3,1,4,128]{4,3,2,1,0:T(4,128)S(1)}, f32[3,3,1,4,128]{4,3,2,1,0:T(4,128)S(1)}, u32[]{:S(2)}, u32[]{:S(2)}) collective-permute-start(f32[3,3,1,4,128]{4,3,2,1,0:T(4,128)S(1)} %get-tuple-element.575), channel_id=1, source_target_pairs={{0,4},{4,8},{8,12},{12,0},{1,5},{5,9},{9,13},{13,1},{2,6},{6,10},{... | collective-permute-start | bytes 55304 | tf_op jit(solution)/shard_map/ppermute | solution.py:23
  152.9 3.7 collective-permute-start.12
  153.9 3.7 collective-permute-start.13
  157.6 9.6 %collective-permute-start.14 = (f32[3,1,4,128]{3,2,1,0:T(4,128)S(1)}, f32[3,1,4,128]{3,2,1,0:T(4,128)S(1)}, u32[]{:S(2)}, u32[]{:S(2)}) collective-permute-start(f32[3,1,4,128]{3,2,1,0:T(4,128)S(1)} %get-tuple-element.644), channel_id=1, source_target_pairs={{4,0},{8,4},{12,8},{0,12},{5,1},{9,5},{13,9},{1,13},{6,2},{10,6},{... | collective-permute-start | bytes 18440 | tf_op jit(solution)/shard_map/ppermute | solution.py:24
  159.6 9.5 %collective-permute-start.15 = (f32[3,1,4,128]{3,2,1,0:T(4,128)S(1)}, f32[3,1,4,128]{3,2,1,0:T(4,128)S(1)}, u32[]{:S(2)}, u32[]{:S(2)}) collective-permute-start(f32[3,1,4,128]{3,2,1,0:T(4,128)S(1)} %get-tuple-element.643), channel_id=1, source_target_pairs={{0,4},{4,8},{8,12},{12,0},{1,5},{5,9},{9,13},{13,1},{2,6},{6,10},{... | collective-permute-start | bytes 18440 | tf_op jit(solution)/shard_map/ppermute | solution.py:23
  218.7 4.0 collective-permute-start.18
  221.1 3.7 collective-permute-start.19
  227.0 5.4 collective-permute-start.21
  283.4 4.0 collective-permute-start.24
  285.7 3.7 collective-permute-start.25
  289.4 4.5 collective-permute-start.26
  291.6 5.4 collective-permute-start.27
  347.7 4.0 collective-permute-start.30
  350.0 3.7 collective-permute-start.31
  353.7 4.2 collective-permute-start.32
  356.0 5.4 collective-permute-start.33
  411.6 4.0 collective-permute-start.36
  414.0 3.7 collective-permute-start.37
  417.6 82.4 %collective-permute-start.38 = (f32[3,1,4,128]{3,2,1,0:T(4,128)S(1)}, f32[3,1,4,128]{3,2,1,0:T(4,128)S(1)}, u32[]{:S(2)}, u32[]{:S(2)}) collective-permute-start(f32[3,1,4,128]{3,2,1,0:T(4,128)S(1)} %get-tuple-element.636), channel_id=1, source_target_pairs={{4,0},{8,4},{12,8},{0,12},{5,1},{9,5},{13,9},{1,13},{6,2},{10,6},{... | collective-permute-start | bytes 18440 | tf_op jit(solution)/shard_map/ppermute | solution.py:24
  419.9 80.1 %collective-permute-start.39 = (f32[3,1,4,128]{3,2,1,0:T(4,128)S(1)}, f32[3,1,4,128]{3,2,1,0:T(4,128)S(1)}, u32[]{:S(2)}, u32[]{:S(2)}) collective-permute-start(f32[3,1,4,128]{3,2,1,0:T(4,128)S(1)} %get-tuple-element.635), channel_id=1, source_target_pairs={{0,4},{4,8},{8,12},{12,0},{1,5},{5,9},{9,13},{13,1},{2,6},{6,10},{... | collective-permute-start | bytes 18440 | tf_op jit(solution)/shard_map/ppermute | solution.py:23
  495.5 13.1 %all-to-all-start.3 = ((f32[8,64,128]{2,1,0:T(8,128)}), f32[8,64,128]{2,1,0:T(8,128)S(1)}, u32[]{:S(2)}, u32[]{:S(2)}) async-start(f32[8,64,128]{2,1,0:T(8,128)} %bitcast.133), calls=%async_computation.3 | async-start | bytes 524288 | tf_op jit(solution)/shard_map/all_to_all | solution.py:209
  511.7 10.4 %all-to-all-start.4 = ((f32[8,1,384]{2,1,0:T(1,128)}), f32[8,1,384]{2,1,0:T(1,128)S(1)}, u32[]{:S(2)}, u32[]{:S(2)}) async-start(f32[8,1,384]{2,1,0:T(1,128)} %reshape.2469), calls=%async_computation.4 | async-start | bytes 24576 | tf_op jit(solution)/shard_map/all_to_all | solution.py:98
  580.8 3.7 collective-permute-start.42
  581.4 3.7 collective-permute-start.43
  585.7 5.4 collective-permute-start.45
  640.2 4.0 collective-permute-start.48
  642.5 3.7 collective-permute-start.49
  646.2 3.9 collective-permute-start.50
  647.9 5.4 collective-permute-start.51
  704.5 4.0 collective-permute-start.54
  710.5 4.2 collective-permute-start.56
  712.8 5.4 collective-permute-start.57
  768.8 4.0 collective-permute-start.60
  771.1 3.7 collective-permute-start.61
  774.8 4.5 collective-permute-start.62
  777.1 5.4 collective-permute-start.63
  (29 other events, 165.2 us)
where the time goes:
time: 924 us; the launch traced here: 914 us
  blocking collectives  317 us (34%)
  other arithmetic  253 us (27%)
  waiting for transfers between devices  131 us (14%)
  starting transfers between devices  94.8 us (10%)
  local copies, waits for them, and re-layouts  84.8 us (9%)
  between operations  28.7 us (3%)
    psum x8, blocking collectives, paired_sums(): lax.psum((jnp.sum(residual * precond), jnp.sum(image * precond)), ('flow'...  303 us
    reduce_sum x32, other arithmetic, one_group(): result = jnp.sum(weight * rate[:, None, :], axis=-1)  82.9 us
    reduce_sum x32, other arithmetic, one_group(): result = jnp.sum(weight * field_rows[where][:, :, None], axis=1)  81.2 us
    ppermute x33, waiting for transfers between devices, padded_2(): before = lax.ppermute(last, axis, up)  65.3 us
    ppermute x33, waiting for transfers between devices, padded_2(): after = lax.ppermute(initial, axis, down)  59 us
    reduce_sum x20, other arithmetic, pair_kernel(): return jnp.sum(weight * values[..., None, :], axis=-1)  53.7 us
    ppermute x33, starting transfers between devices, padded_2(): after = lax.ppermute(initial, axis, down)  49.1 us
    gather x64, local copies, waits for them, and re-layouts, one_group(): weight = marker_weights(fluid_rows[where], positions)  39 us
  transfers between devices with their start and end apart: 71, of which 59 were waited for; matrix products, arithmetic and copies ran while one was open for 12% of the time, Pallas kernels for 0%

commit v1 on v0

v1 whole, which is shorter than its diff:
```python
import functools
import math

import jax
import jax.numpy as jnp
from jax import lax
from jax.experimental import pallas as pl
from jax.experimental.pallas import tpu as pltpu
from jax.sharding import PartitionSpec as P

ITERS = 4
STEPS = 2
STIFFEN = 0.5
STEP_TIME = 0.05
PER_PARTICLE = 1.0 / 128.0
SCALE = math.sqrt(math.log2(math.e))
SHIFT = math.log2(PER_PARTICLE)
MESH = pl.DeviceIdType.MESH
HIGHEST = lax.Precision.HIGHEST
CHUNK = 32
COLS = 8


def weight_of(gaps):
    total = None
    for gap in gaps:
        total = gap * gap if total is None else total + gap * gap
    return jnp.exp2(SHIFT - total)


def solve_small(gram, right):
    n = len(right)
    gram = [list(row) for row in gram]
    right = list(right)
    for i in range(n):
        inverse = 1.0 / gram[i][i]
        for j in range(i + 1, n):
            factor = gram[j][i] * inverse
            for k in range(i + 1, n):
                gram[j][k] = gram[j][k] - factor * gram[i][k]
            right[j] = right[j] - factor * right[i]
    out = [None] * n
    for i in reversed(range(n)):
        value = right[i]
        for k in range(i + 1, n):
            value = value - gram[i][k] * out[k]
        out[i] = value / gram[i][i]
    return out


def kernel(
    sizes,
    dims,
    slot_ref,
    cell_ref,
    off_ref,
    source_ref,
    geo_ref,
    start_ref,
    mass_ref,
    column_ref,
    row_ref,
    press_out,
    speed_out,
    off_group,
    off_depth,
    weights,
    geo_turned,
    shift_rows,
    normal_sums,
    give,
    take,
    krylov,
    krylov_depth,
    part_group,
    part_depth,
    off_send,
    off_recv,
    take_send,
    take_recv,
    kry_send,
    kry_recv,
    part_send,
    part_recv,
):
    n_flow, n_cross, n_depth = sizes
    size_x, size_y, size_z = dims
    cells = size_x * size_y * size_z
    tiles = n_flow * n_cross
    grains = geo_ref.shape[0]
    blocks = column_ref.shape[0]
    per_grain = blocks // grains
    lanes = off_ref.shape[-1]
    flow, cross, depth = (lax.axis_index("flow"), lax.axis_index("cross"), lax.axis_index("depth"))

    def group_at(slot):
        rf, rc = divmod(slot, n_cross)
        return (lax.rem(flow + rf, n_flow), lax.rem(cross + rc, n_cross), depth)

    def group_back(slot):
        rf, rc = divmod(slot, n_cross)
        return (
            lax.rem(flow + n_flow - rf, n_flow),
            lax.rem(cross + n_cross - rc, n_cross),
            depth,
        )

    def depth_at(rd):
        return (flow, cross, lax.rem(depth + rd, n_depth))

    slot_flow = {1: (n_flow - 1) * n_cross, -1: (1 % n_flow) * n_cross}
    slot_cross = {1: n_cross - 1, -1: 1 % n_cross}
    near_slots = sorted({slot_flow[1], slot_flow[-1], slot_cross[1], slot_cross[-1]} - {0})
    far_slots = [r for r in range(1, tiles) if r not in near_slots]
    near_slots = sorted(near_slots, key=lambda r: r // n_cross)
    order = near_slots + far_slots
    near_depth = sorted({1, n_depth - 1})
    depth_index = {1: near_depth.index(n_depth - 1), -1: near_depth.index(1)}

    barrier = pltpu.get_barrier_semaphore()
    for r in range(1, tiles):
        pl.semaphore_signal(barrier, inc=1, device_id=group_at(r), device_id_type=MESH)
    for rd in range(1, n_depth):
        pl.semaphore_signal(barrier, inc=1, device_id=depth_at(rd), device_id_type=MESH)
    pl.semaphore_wait(barrier, tiles - 1 + n_depth - 1)

    sent = []

    def ship(src, dst, send_sem, recv_sem, device):
        copy = pltpu.make_async_remote_copy(
            src_ref=src,
            dst_ref=dst,
            send_sem=send_sem,
            recv_sem=recv_sem,
            device_id=device,
            device_id_type=MESH,
        )
        copy.start()
        sent.append(copy)
        return copy

    off_copies = {}
    for r in order:
        off_copies[r] = ship(
            off_ref, off_group.at[r], off_send.at[r], off_recv.at[r], group_at(r)
        )
    off_depth_copies = []
    for i, rd in enumerate(near_depth):
        off_depth_copies.append(
            ship(
                off_ref,
                off_depth.at[i],
                off_send.at[tiles + i],
                off_recv.at[tiles + i],
                depth_at(rd),
            )
        )
    off_group[0] = off_ref[...]

    def turn(g, carry):
        geo_turned[g] = jnp.transpose(geo_ref[g])
        return carry

    lax.fori_loop(0, grains, turn, 0)
    for r in order:
        off_copies[r].wait_recv()

    one_hot_row = (
        lax.broadcasted_iota(jnp.int32, (tiles * cells, blocks), 0) == row_ref[...]
    ).astype(jnp.float32)

    def marker_pass(g, carry):
        shift = shift_rows[pl.ds(g, 1), :]
        rows = [[], [], []]
        for b in range(per_grain):
            slot = slot_ref[g * per_grain + b]
            cell = cell_ref[g * per_grain + b]
            own = [off_group[slot, pl.ds(c * cells + cell, 1), :] for c in range(3)]
            sums = [None, None, None]
            for low in range(0, lanes, CHUNK):
                piece = geo_turned[g, low : low + CHUNK, :] + shift
                weight = weight_of(
                    [piece[:, b * COLS + c : b * COLS + c + 1] - own[c] for c in range(3)]
                )
                for c in range(3):
                    term = piece[:, b * COLS + 3 + c : b * COLS + 4 + c] * weight
                    term = jnp.sum(term.reshape(CHUNK // 8, 8, lanes), axis=0)
                    sums[c] = term if sums[c] is None else sums[c] + term
            for c in range(3):
                rows[c].append(jnp.sum(sums[c], axis=0, keepdims=True))
        for c in range(3):
            normal_sums[c, pl.ds(pl.multiple_of(g * per_grain, 8), per_grain), :] = jnp.concatenate(
                rows[c], axis=0
            )
        return carry

    lane = lax.rem(lax.broadcasted_iota(jnp.int32, (grains, lanes), 1), COLS)
    speed = start_ref[...]
    moved = jnp.zeros((grains, lanes), jnp.float32)
    velocity = [jnp.broadcast_to(speed[:, c : c + 1], (grains, lanes)) for c in range(3)]
    displace = [moved, moved, moved]

    def to_fluid(step):
        added = None
        for c in range(3):
            term = normal_sums[c].reshape(grains, per_grain, lanes) * velocity[c][:, None, :]
            added = term if added is None else added + term
        spread = jnp.dot(
            one_hot_row,
            added.reshape(blocks, lanes),
            precision=HIGHEST,
            preferred_element_type=jnp.float32,
        )
        give[step] = spread.reshape(tiles, cells, lanes)
        return [
            ship(
                give.at[step, r],
                take.at[step, r],
                take_send.at[step, r],
                take_recv.at[step, r],
                group_back(r),
            )
            for r in reversed(order)
        ]

    def collect(step, copies):
        total = give[step, 0]
        for copy in copies:
            copy.wait_recv()
        for r in range(1, tiles):
            total = total + take[step, r]
        return total

    merged = size_x == 1 and n_flow == 2
    sources = {("own", 0): 0}
    flow_keys = [("flow", 1)] if merged else [("flow", 1), ("flow", -1)]
    for key in flow_keys + [("cross", 1), ("cross", -1), ("depth", 1), ("depth", -1)]:
        sources[key] = len(sources)
    padded_rows = -(-len(sources) * cells // 128) * 128

    def columns_of(pick):
        rows = []
        for axis, side in sources:
            if axis == "own":
                rows.append(pick(0, None))
            elif axis == "flow":
                rows.append(pick(slot_flow[side], None))
            elif axis == "cross":
                rows.append(pick(slot_cross[side], None))
            else:
                rows.append(pick(None, depth_index[side]))
        spare = padded_rows - len(sources) * cells
        if spare:
            rows.append(jnp.zeros((spare, lanes), jnp.float32))
        return jnp.transpose(jnp.concatenate(rows, axis=0))

    def pairs(cell):
        x, rest = divmod(cell, size_y * size_z)
        y, z = divmod(rest, size_z)
        found = [(cell, (0, 0, 0))]
        place, extent, names = (x, y, z), (size_x, size_y, size_z), ("flow", "cross", "depth")
        for axis in range(3):
            for side in (1, -1):
                near = list(place)
                near[axis] += side
                key = ("own", 0)
                if not 0 <= near[axis] < extent[axis]:
                    near[axis] %= extent[axis]
                    key = (names[axis], side)
                    if axis == 0 and merged:
                        key = (names[axis], 1)
                index = (near[0] * size_y + near[1]) * size_z + near[2]
                step = [0, 0, 0]
                step[axis] = side
                found.append((sources[key] * cells + index, tuple(step)))
        return found

    groups = []
    for cell in range(cells):
        by_column = {}
        for column, step in pairs(cell):
            by_column.setdefault(column, []).append(step)
        groups.append(list(by_column.items()))

    shift_rows[...] = moved
    lax.fori_loop(0, grains, marker_pass, 0)
    copies = to_fluid(0)
    for copy in off_depth_copies:
        copy.wait_recv()

    turned = [
        columns_of(
            lambda slot, i, c=c: (
                off_group[slot, c * cells : (c + 1) * cells, :]
                if i is None
                else off_depth[i, c * cells : (c + 1) * cells, :]
            )
        )
        for c in range(3)
    ]
    sum_rows = []
    for cell in range(cells):
        own = [off_ref[c * cells + cell : c * cells + cell + 1, :] for c in range(3)]
        full = None
        for position, (column, steps) in enumerate(groups[cell]):
            total = None
            for step in steps:
                weight = weight_of(
                    [
                        turned[c][:, column : column + 1] - (own[c] - SCALE * step[c])
                        for c in range(3)
                    ]
                )
                total = weight if total is None else total + weight
            weights[cell, position] = total
            full = total if full is None else full + total
        sum_rows.append(jnp.sum(full, axis=0, keepdims=True))
    rowsum = jnp.concatenate(sum_rows, axis=0)
    diagonal = STIFFEN + rowsum - PER_PARTICLE
    inverse = 1.0 / diagonal

    def weighted(step, j):
        turned_field = columns_of(
            lambda slot, i: krylov[step, j, slot] if i is None else krylov_depth[step, j, i]
        )
        rows = []
        for cell in range(cells):
            total = None
            for low in range(0, lanes, 64):
                acc = None
                for position, (column, _) in enumerate(groups[cell]):
                    term = (
                        weights[cell, position, low : low + 64, :]
                        * turned_field[low : low + 64, column : column + 1]
                    )
                    acc = term if acc is None else acc + term
                acc = jnp.sum(acc.reshape(8, 8, lanes), axis=0)
                total = acc if total is None else total + acc
            rows.append(jnp.sum(total, axis=0, keepdims=True))
        return jnp.concatenate(rows, axis=0)

    pressure = jnp.zeros((cells, lanes), jnp.float32)
    spread_before = None
    residual = None
    pressure_all = None
    one_hot_column = (
        lax.broadcasted_iota(jnp.int32, (blocks, tiles * cells), 1) == column_ref[...]
    ).astype(jnp.float32)
    for step in range(STEPS):
        if step:
            shift_rows[...] = moved * SCALE
            lax.fori_loop(0, grains, marker_pass, 0)
            copies = to_fluid(step)
        spread = collect(step, copies)
        if step == 0:
            residual = source_ref[...] + spread
        else:
            residual = residual + (spread - spread_before)
        spread_before = spread
        fields = [residual * inverse]
        far = []
        for j in range(ITERS):
            krylov[step, j, 0] = fields[j]
            near = {}
            for r in near_slots:
                near[r] = ship(
                    krylov.at[step, j, 0],
                    krylov.at[step, j, r],
                    kry_send.at[step, j, r],
                    kry_recv.at[step, j, r],
                    group_at(r),
                )
            beside = [
                ship(
                    krylov.at[step, j, 0],
                    krylov_depth.at[step, j, i],
                    kry_send.at[step, j, tiles + i],
                    kry_recv.at[step, j, tiles + i],
                    depth_at(rd),
                )
                for i, rd in enumerate(near_depth)
            ]
            for r in far_slots:
                far.append(
                    ship(
                        krylov.at[step, j, 0],
                        krylov.at[step, j, r],
                        kry_send.at[step, j, r],
                        kry_recv.at[step, j, r],
                        group_at(r),
                    )
                )
            for copy in list(near.values()) + beside:
                copy.wait_recv()
            fields.append((weighted(step, j) - PER_PARTICLE * fields[j]) * inverse)
        moments = []
        for j in range(ITERS):
            scaled = diagonal * fields[j]
            moments.append(jnp.sum(scaled * fields[j], axis=0, keepdims=True))
            moments.append(jnp.sum(scaled * fields[j + 1], axis=0, keepdims=True))
        part_group[step, 0] = jnp.concatenate(moments, axis=0)
        waits = [
            ship(
                part_group.at[step, 0],
                part_group.at[step, r],
                part_send.at[step, r],
                part_recv.at[step, r],
                group_at(r),
            )
            for r in order
        ]
        for copy in waits:
            copy.wait_recv()
        total = part_group[step, 0]
        for r in range(1, tiles):
            total = total + part_group[step, r]
        part_depth[step, 0] = total
        waits = [
            ship(
                part_depth.at[step, 0],
                part_depth.at[step, rd],
                part_send.at[step, tiles + rd],
                part_recv.at[step, tiles + rd],
                depth_at(rd),
            )
            for rd in range(1, n_depth)
        ]
        for copy in waits:
            copy.wait_recv()
        for rd in range(1, n_depth):
            total = total + part_depth[step, rd]
        total = jnp.broadcast_to(jnp.sum(total, axis=1, keepdims=True), total.shape)
        scalars = [total[q : q + 1, :] for q in range(2 * ITERS)]
        gram = [
            [scalars[i + j] - scalars[i + j + 1] for j in range(ITERS)] for i in range(ITERS)
        ]
        factors = solve_small(gram, scalars[:ITERS])
        for j in range(ITERS):
            pressure = pressure + factors[j] * fields[j]
            residual = residual - factors[j] * (diagonal * (fields[j] - fields[j + 1]))
        for copy in far:
            copy.wait_recv()
        for j in range(ITERS):
            term = factors[j] * krylov[step, j].reshape(tiles * cells, lanes)
            pressure_all = term if pressure_all is None else pressure_all + term
        felt = jnp.dot(
            one_hot_column,
            pressure_all,
            precision=HIGHEST,
            preferred_element_type=jnp.float32,
        )
        moved = jnp.zeros((grains, lanes), jnp.float32)
        for c in range(3):
            force = (normal_sums[c] * felt).reshape(grains, per_grain, lanes)
            force = jnp.sum(jnp.sum(force, axis=1), axis=1, keepdims=True)
            velocity[c] = velocity[c] + STEP_TIME * force / mass_ref[...]
            displace[c] = displace[c] + STEP_TIME * velocity[c]
            moved = jnp.where(lane == c, displace[c], moved)
    press_out[...] = pressure
    speed = jnp.zeros((grains, lanes), jnp.float32)
    for c in range(3):
        speed = jnp.where(lane == c, velocity[c], speed)
    speed_out[...] = speed
    for copy in sent:
        copy.wait_send()


def per_device(
    sizes,
    fluid_offsets,
    source,
    marker_offsets,
    marker_normals,
    dest_tile,
    cell_index,
    grain_velocity,
    grain_mass,
):
    n_flow, n_cross, n_depth = sizes
    tiles = n_flow * n_cross
    dims = source.shape[:3]
    cells = dims[0] * dims[1] * dims[2]
    lanes = source.shape[3]
    grains, per_grain = cell_index.shape
    blocks = grains * per_grain
    tile = dest_tile.reshape(blocks)
    slot_flow = (lax.axis_index("flow") - tile // n_cross) % n_flow
    slot_cross = (lax.axis_index("cross") - tile % n_cross) % n_cross
    slot = (slot_flow * n_cross + slot_cross).astype(jnp.int32)
    cell = cell_index.reshape(blocks)
    place = slot * cells + cell
    offsets = (fluid_offsets * SCALE).reshape(3 * cells, lanes)
    geometry = jnp.concatenate(
        [
            marker_offsets * SCALE,
            marker_normals,
            jnp.zeros((grains, per_grain, COLS - 6, lanes), jnp.float32),
        ],
        axis=2,
    ).reshape(grains, per_grain * COLS, lanes)
    start = jnp.pad(grain_velocity, ((0, 0), (0, lanes - 3)))
    mass = jnp.broadcast_to(grain_mass[:, None], (grains, lanes))
    near_count = len({1, n_depth - 1})
    vmem, dma = pltpu.VMEM, pltpu.SemaphoreType.DMA
    f32 = jnp.float32
    in_vmem = pl.BlockSpec(memory_space=pltpu.VMEM)
    in_smem = pl.BlockSpec(memory_space=pltpu.SMEM)
    pressure, speed = pl.pallas_call(
        functools.partial(kernel, sizes, dims),
        out_shape=(
            jax.ShapeDtypeStruct((cells, lanes), f32),
            jax.ShapeDtypeStruct((grains, lanes), f32),
        ),
        in_specs=[in_smem] * 2 + [in_vmem] * 7,
        out_specs=(in_vmem, in_vmem),
        scratch_shapes=[
            vmem((tiles, 3 * cells, lanes), f32),
            vmem((near_count, 3 * cells, lanes), f32),
            vmem((cells, 7, lanes, lanes), f32),
            vmem((grains, lanes, per_grain * COLS), f32),
            vmem((grains, lanes), f32),
            vmem((3, blocks, lanes), f32),
            vmem((STEPS, tiles, cells, lanes), f32),
            vmem((STEPS, tiles, cells, lanes), f32),
            vmem((STEPS, ITERS, tiles, cells, lanes), f32),
            vmem((STEPS, ITERS, near_count, cells, lanes), f32),
            vmem((STEPS, tiles, 2 * ITERS, lanes), f32),
            vmem((STEPS, n_depth, 2 * ITERS, lanes), f32),
            dma((tiles + near_count,)),
            dma((tiles + near_count,)),
            dma((STEPS, tiles)),
            dma((STEPS, tiles)),
            dma((STEPS, ITERS, tiles + near_count)),
            dma((STEPS, ITERS, tiles + near_count)),
            dma((STEPS, tiles + n_depth)),
            dma((STEPS, tiles + n_depth)),
        ],
        compiler_params=pltpu.CompilerParams(
            collective_id=0, has_side_effects=True, vmem_limit_bytes=56 * 1024 * 1024
        ),
        name="coupled",
    )(
        slot,
        cell,
        offsets,
        source.reshape(cells, lanes),
        geometry,
        start,
        mass,
        place[:, None],
        place[None, :],
    )
    return (pressure.reshape(source.shape), speed[:, :3])


def solution(mesh):
    sizes = tuple(mesh.shape[name] for name in ("flow", "cross", "depth"))
    return jax.shard_map(
        functools.partial(per_device, sizes),
        mesh=mesh,
        in_specs=(
            P(None, "flow", "cross", "depth", None),
            P("flow", "cross", "depth", None),
            P(("flow", "cross", "depth"), None, None, None),
            P(("flow", "cross", "depth"), None, None, None),
            P(("flow", "cross", "depth"), None, None),
            P(("flow", "cross", "depth"), None),
            P(("flow", "cross", "depth"), None),
            P(("flow", "cross", "depth")),
        ),
        out_specs=(P("flow", "cross", "depth", None), P(("flow", "cross", "depth"), None)),
        check_vma=False,
    )
```

time: 924 us -> 167 us (0.18); the launches traced: 914 us -> 167 us
  blocking collectives: 317 us -> 0 us
  other arithmetic: 253 us -> 5.31 us
  Pallas kernels: 0 us -> 154 us
  waiting for transfers between devices: 131 us -> 0 us
  starting transfers between devices: 94.8 us -> 0 us
  local copies, waits for them, and re-layouts: 84.8 us -> 7.08 us
  between operations: 28.7 us -> 0.71 us
    psum x8 -> x0, blocking collectives: 303 us -> none  [paired_sums(): lax.psum((jnp.sum(residual * precond), jnp.sum(image * precond)), ('flow'...]
    reduce_sum x95 -> x0, other arithmetic: 223 us -> none  [the longest x32 82.9 us: one_group(): result = jnp.sum(weight * rate[:, None, :], axis=-1)]
    pallas_call x0 -> x1, Pallas kernels: none -> 154 us  [per_device(): pl.pallas_call(functools.partial(kernel, sizes, dims), out_shape=(jax.Sha...]
    ppermute x66 -> x0, waiting for transfers between devices: 124 us -> none  [the longest x33 65.3 us: padded_2(): before = lax.ppermute(last, axis, up)]
    ppermute x66 -> x0, starting transfers between devices: 70.5 us -> none  [the longest x33 49.1 us: padded_2(): after = lax.ppermute(initial, axis, down)]
    gather x98 -> x0, local copies, waits for them, and re-layouts: 58.8 us -> none  [the longest x64 39 us: one_group(): weight = marker_weights(fluid_rows[where], positions)]
    all_to_all x5 -> x0, starting transfers between devices: 24.2 us -> none  [the longest x2 9.86 us: send_markers(): lax.all_to_all(motion_buffer, ('flow', 'cross'), split_axis=0, concat_axi...]
    dynamic_update_slice x64 -> x0, other arithmetic: 14.5 us -> none  [marker_pass(): return lax.map(one_group, pieces).reshape(slot_count, 128)]
  transfers between devices with their start and end apart: 71 -> 0, of which waited for: 59 -> 0; matrix products, arithmetic and copies ran while one was open for 12% -> 0% of each run, Pallas kernels for 0% -> 0%
where the time goes in v1:
time: 167 us
  Pallas kernels  154 us (92%)
  local copies, waits for them, and re-layouts  7.08 us (4%)
  other arithmetic  5.31 us (3%)
    pallas_call x1, Pallas kernels, per_device(): pl.pallas_call(functools.partial(kernel, sizes, dims), out_shape=(jax.Sha...  154 us

profile of v1, /device:TPU:0, one launch (start us, length us, event | category | flops | bytes accessed | tf_op | source)
XLA Modules:
  0.0 166.7 jit_solution(1698795152418102727)
XLA Ops:
  0.6 0.5 broadcast.373
  1.1 0.0 copy-start.3
  1.1 1.4 reduce.7
  2.5 0.1 reshape.403
  2.6 0.0 copy-start.1
  2.6 0.6 fusion.10.slot_ref
  3.2 0.1 copy-done.1
  3.3 0.7 reshape.404.cell_ref
  4.0 0.0 copy-done.3
  4.0 0.6 broadcast_multiply_fusion.1
  4.6 0.0 copy-start
  4.6 1.1 broadcast_multiply_fusion
  5.7 0.1 pad.7.clone
  5.8 0.0 copy-done
  5.8 0.2 maximum_maximum_fusion
  5.9 0.0 copy-start.5
  5.9 1.3 copy.22
  7.3 0.0 copy-done.5
  7.3 0.1 copy.14
  7.3 0.0 copy-start.6
  7.3 0.6 pad.4.start_ref
  8.0 0.1 copy-done.6
  8.0 0.7 broadcast_in_dim.5.mass_ref
  8.7 0.0 copy-start.2
  8.7 0.1 reshape.414
  8.8 0.6 copy-done.2
  9.4 0.1 reshape.413
  9.5 0.9 fusion.5.column_ref
  10.4 0.1 reshape.411
  10.4 0.1 reshape.410
  10.5 0.6 multiply_add_fusion.row_ref
  11.1 153.6 %coupled.1 = (f32[16,128]{1,0:T(8,128)}, f32[16,128]{1,0:T(8,128)}) custom-call(s32[256]{0:T(256)} %fusion.10.slot_ref, s32[256]{0:T(256)} %reshape.404.cell_ref, f32[48,128]{1,0:T(8,128)} %bitcast.10, f32[16,128]{1,0:T(8,128)} %bitcast.13, f32[16,128,128]{2,1,0:T(8,128)} %bitcast.9, f32[16,128]{1,0:T(8,128)} %pad.4.start_ref, ...), custom_call_target="tpu_custom_call" | custom-call | tf_op jit(solution)/shard_map/coupled/pallas_call | solution.py:508
  164.8 0.0 copy-start.4
  164.8 1.4 copy.20
  166.1 0.0 copy-done.4
  166.1 0.6 copy.24
  (1 shorter events, 0.0 us)
Async XLA Ops:
  1.1 2.8 %copy-start.3 = (f32[3,1,4,4,128]{4,3,2,1,0:T(4,128)S(1)}, f32[3,1,4,4,128]{4,3,2,1,0:T(4,128)}, u32[]{:S(2)}) copy-start(f32[3,1,4,4,128]{4,3,2,1,0:T(4,128)} %param.8) | copy-start | bytes 73732
  2.6 0.7 copy-start.1
  4.6 1.2 copy-start
  5.9 1.3 copy-start.5
  7.3 0.7 copy-start.6
  8.7 0.7 copy-start.2
  164.8 1.4 copy-start.4

commit v2 on v1

--- a/solution.py
+++ b/solution.py
@@ -17,7 +17,6 @@
 SHIFT = math.log2(PER_PARTICLE)
 MESH = pl.DeviceIdType.MESH
 HIGHEST = lax.Precision.HIGHEST
-CHUNK = 32
 COLS = 8
 
 
@@ -26,6 +25,16 @@
     for gap in gaps:
         total = gap * gap if total is None else total + gap * gap
     return jnp.exp2(SHIFT - total)
+
+
+def rounded(value):
+    return value.astype(jnp.bfloat16).astype(jnp.float32)
+
+
+def three_parts(value):
+    high = rounded(value)
+    middle = rounded(value - high)
+    return high, middle, (value - high) - middle
 
 
 def solve_small(gram, right):
@@ -66,6 +75,7 @@
     off_depth,
     weights,
     geo_turned,
+    own_features,
     shift_rows,
     normal_sums,
     give,
@@ -157,40 +167,75 @@
         )
     off_group[0] = off_ref[...]
 
+    part = lax.rem(lax.broadcasted_iota(jnp.int32, (per_grain * COLS, lanes), 0), COLS)
+    row = lax.broadcasted_iota(jnp.int32, (COLS, lanes), 0)
+    block_lane = lax.broadcasted_iota(jnp.int32, (lanes, per_grain * COLS), 1) // COLS
+
     def turn(g, carry):
-        geo_turned[g] = jnp.transpose(geo_ref[g])
+        rows = geo_ref[g]
+        high = rounded(rows)
+        low = rows - high
+        low = jnp.concatenate([low[3:], low[:3]], axis=0)
+        mix = jnp.where(part < 3, low, jnp.where(part < 6, high, 0.0))
+        geo_turned[g] = jnp.transpose(mix)
+        return carry
+
+    def own_pass(slot, carry):
+        done = []
+        for cell in range(cells):
+            own = [off_group[slot, c * cells + cell : c * cells + cell + 1, :] for c in range(3)]
+            square = own[0] * own[0] + own[1] * own[1] + own[2] * own[2] - SHIFT
+            base = jnp.where(row == 4, -square, 0.0)
+            for c in range(3):
+                base = jnp.where(row == c, 2.0 * own[c], base)
+            high, middle, low = three_parts(base)
+            high = jnp.where(row == 3, -1.0, high)
+            features = jnp.concatenate([high, middle, low, high, middle, high], axis=0)
+            done.append(jnp.transpose(features).astype(jnp.bfloat16))
+        for cell in range(cells):
+            own_features[slot * cells + cell] = done[cell]
         return carry
 
     lax.fori_loop(0, grains, turn, 0)
     for r in order:
         off_copies[r].wait_recv()
+    lax.fori_loop(0, tiles, own_pass, 0)
 
     one_hot_row = (
         lax.broadcasted_iota(jnp.int32, (tiles * cells, blocks), 0) == row_ref[...]
     ).astype(jnp.float32)
 
     def marker_pass(g, carry):
-        shift = shift_rows[pl.ds(g, 1), :]
-        rows = [[], [], []]
+        shift = shift_rows[g]
+        turned = geo_turned[g]
+        total = None
         for b in range(per_grain):
-            slot = slot_ref[g * per_grain + b]
-            cell = cell_ref[g * per_grain + b]
-            own = [off_group[slot, pl.ds(c * cells + cell, 1), :] for c in range(3)]
-            sums = [None, None, None]
-            for low in range(0, lanes, CHUNK):
-                piece = geo_turned[g, low : low + CHUNK, :] + shift
-                weight = weight_of(
-                    [piece[:, b * COLS + c : b * COLS + c + 1] - own[c] for c in range(3)]
+            place = slot_ref[g * per_grain + b] * cells + cell_ref[g * per_grain + b]
+            point = jnp.where(row < 3, geo_ref[g, b * COLS : (b + 1) * COLS, :] + shift, 0.0)
+            square = jnp.sum(point * point, axis=0, keepdims=True)
+            point = jnp.where(row == 3, square, jnp.where(row == 4, 1.0, point))
+            high, middle, low = three_parts(point)
+            features = jnp.concatenate([high, high, high, middle, middle, low], axis=0)
+            weight = jnp.exp2(
+                jnp.dot(
+                    own_features[place],
+                    features.astype(jnp.bfloat16),
+                    preferred_element_type=jnp.float32,
                 )
-                for c in range(3):
-                    term = piece[:, b * COLS + 3 + c : b * COLS + 4 + c] * weight
-                    term = jnp.sum(term.reshape(CHUNK // 8, 8, lanes), axis=0)
-                    sums[c] = term if sums[c] is None else sums[c] + term
-            for c in range(3):
-                rows[c].append(jnp.sum(sums[c], axis=0, keepdims=True))
+            )
+            upper = weight.astype(jnp.bfloat16)
+            lower = (weight - upper.astype(jnp.float32)).astype(jnp.bfloat16)
+            normals = jnp.where(block_lane == b, turned, 0.0).astype(jnp.bfloat16)
+            term = jnp.dot(
+                jnp.concatenate([upper, lower], axis=1),
+                jnp.concatenate([normals, normals], axis=0),
+                preferred_element_type=jnp.float32,
+            )
+            total = term if total is None else total + term
+        total = jnp.transpose(total).reshape(per_grain, COLS, lanes)
         for c in range(3):
-            normal_sums[c, pl.ds(pl.multiple_of(g * per_grain, 8), per_grain), :] = jnp.concatenate(
-                rows[c], axis=0
+            normal_sums[c, pl.ds(pl.multiple_of(g * per_grain, 8), per_grain), :] = (
+                total[:, c, :] + total[:, c + 3, :]
             )
         return carry
 
@@ -282,7 +327,7 @@
             by_column.setdefault(column, []).append(step)
         groups.append(list(by_column.items()))
 
-    shift_rows[...] = moved
+    shift_rows[...] = jnp.zeros(shift_rows.shape, jnp.float32)
     lax.fori_loop(0, grains, marker_pass, 0)
     copies = to_fluid(0)
     for copy in off_depth_copies:
@@ -348,7 +393,11 @@
     ).astype(jnp.float32)
     for step in range(STEPS):
         if step:
-            shift_rows[...] = moved * SCALE
+            shift = jnp.zeros(shift_rows.shape, jnp.float32)
+            component = lax.broadcasted_iota(jnp.int32, shift_rows.shape, 1)
+            for c in range(3):
+                shift = jnp.where(component == c, SCALE * displace[c][:, None, :], shift)
+            shift_rows[...] = shift
             lax.fori_loop(0, grains, marker_pass, 0)
             copies = to_fluid(step)
         spread = collect(step, copies)
@@ -449,13 +498,11 @@
             precision=HIGHEST,
             preferred_element_type=jnp.float32,
         )
-        moved = jnp.zeros((grains, lanes), jnp.float32)
         for c in range(3):
             force = (normal_sums[c] * felt).reshape(grains, per_grain, lanes)
             force = jnp.sum(jnp.sum(force, axis=1), axis=1, keepdims=True)
             velocity[c] = velocity[c] + STEP_TIME * force / mass_ref[...]
             displace[c] = displace[c] + STEP_TIME * velocity[c]
-            moved = jnp.where(lane == c, displace[c], moved)
     press_out[...] = pressure
     speed = jnp.zeros((grains, lanes), jnp.float32)
     for c in range(3):
@@ -518,7 +565,8 @@
             vmem((near_count, 3 * cells, lanes), f32),
             vmem((cells, 7, lanes, lanes), f32),
             vmem((grains, lanes, per_grain * COLS), f32),
-            vmem((grains, lanes), f32),
+            vmem((tiles * cells, lanes, 6 * COLS), jnp.bfloat16),
+            vmem((grains, COLS, lanes), f32),
             vmem((3, blocks, lanes), f32),
             vmem((STEPS, tiles, cells, lanes), f32),
             vmem((STEPS, tiles, cells, lanes), f32),
@@ -536,7 +584,7 @@
             dma((STEPS, tiles + n_depth)),
         ],
         compiler_params=pltpu.CompilerParams(
-            collective_id=0, has_side_effects=True, vmem_limit_bytes=56 * 1024 * 1024
+            collective_id=0, has_side_effects=True, vmem_limit_bytes=60 * 1024 * 1024
         ),
         name="coupled",
     )(

time: 167 us -> 146 us (0.87)
  Pallas kernels: 154 us -> 132 us
    pallas_call x1, Pallas kernels: 154 us -> 132 us  [per_device(): pl.pallas_call(functools.partial(kernel, sizes, dims), out_shape=(jax.Sha...]
where the time goes in v2:
time: 146 us; the launch traced here: 145 us
  Pallas kernels  132 us (90%)
  local copies, waits for them, and re-layouts  7.08 us (5%)
  other arithmetic  5.31 us (4%)
    pallas_call x1, Pallas kernels, per_device(): pl.pallas_call(functools.partial(kernel, sizes, dims), out_shape=(jax.Sha...  132 us
    unnamed x18, local copies, waits for them, and re-layouts  3.33 us

profile of v2, /device:TPU:0, one launch (start us, length us, event | category | flops | bytes accessed | tf_op | source)
XLA Modules:
  0.0 145.4 jit_solution(13881164702283440082)
XLA Ops:
  0.6 0.5 broadcast.373
  1.1 0.0 copy-start.3
  1.1 1.4 reduce.7
  2.5 0.1 reshape.403
  2.6 0.0 copy-start.1
  2.6 0.6 fusion.10.slot_ref
  3.2 0.1 copy-done.1
  3.3 0.7 reshape.404.cell_ref
  4.0 0.0 copy-done.3
  4.0 0.6 broadcast_multiply_fusion.1
  4.6 0.0 copy-start
  4.6 1.1 broadcast_multiply_fusion
  5.7 0.1 pad.7.clone
  5.8 0.0 copy-done
  5.8 0.2 maximum_maximum_fusion
  5.9 0.0 copy-start.5
  5.9 1.3 copy.22
  7.3 0.0 copy-done.5
  7.3 0.1 copy.14
  7.3 0.0 copy-start.6
  7.3 0.6 pad.4.start_ref
  8.0 0.1 copy-done.6
  8.0 0.7 broadcast_in_dim.5.mass_ref
  8.7 0.0 copy-start.2
  8.7 0.1 reshape.414
  8.8 0.6 copy-done.2
  9.4 0.1 reshape.413
  9.5 0.9 fusion.5.column_ref
  10.4 0.1 reshape.411
  10.4 0.1 reshape.410
  10.5 0.6 multiply_add_fusion.row_ref
  11.1 132.3 %coupled.1 = (f32[16,128]{1,0:T(8,128)}, f32[16,128]{1,0:T(8,128)}) custom-call(s32[256]{0:T(256)} %fusion.10.slot_ref, s32[256]{0:T(256)} %reshape.404.cell_ref, f32[48,128]{1,0:T(8,128)} %bitcast.10, f32[16,128]{1,0:T(8,128)} %bitcast.13, f32[16,128,128]{2,1,0:T(8,128)} %bitcast.9, f32[16,128]{1,0:T(8,128)} %pad.4.start_ref, ...), custom_call_target="tpu_custom_call" | custom-call | tf_op jit(solution)/shard_map/coupled/pallas_call | solution.py:555
  143.4 0.0 copy-start.4
  143.4 1.4 copy.20
  144.8 0.0 copy-done.4
  144.8 0.6 copy.24
  (1 shorter events, 0.0 us)
Async XLA Ops:
  1.1 2.8 %copy-start.3 = (f32[3,1,4,4,128]{4,3,2,1,0:T(4,128)S(1)}, f32[3,1,4,4,128]{4,3,2,1,0:T(4,128)}, u32[]{:S(2)}) copy-start(f32[3,1,4,4,128]{4,3,2,1,0:T(4,128)} %param.8) | copy-start | bytes 73732
  2.6 0.7 copy-start.1
  4.6 1.2 copy-start
  5.9 1.3 copy-start.5
  7.3 0.7 copy-start.6
  8.7 0.7 copy-start.2
  143.4 1.4 copy-start.4
